TPU v7x, 32 devices: a whole 2x2x4 slice. The times are simulated.
32 devices in a mesh: fsdp: 8 (over z, x), pipe: 2 (over core), dp: 2 (over y).
Axes of the slice: x: 2, y: 2, z: 4, core: 2. Of those that a mesh axis runs over, the one named last changes fastest.
Arguments:
- video_tokens: bfloat16 [2, 1024, 2560], P('dp', 'fsdp'), may hold values from -6 to 6
- cached_out: bfloat16 [2, 2, 1024, 2560], P('pipe', 'dp', 'fsdp'), may hold values from -6 to 6
- fresh_mask: int32 [2, 2, 1024], P('pipe', 'dp', 'fsdp'), may hold values from 0 to 1, as said below
- timestep: int32 [2], P('dp'), may hold values from 0 to 49
- up_weight: bfloat16 [2, 7168, 2560], P('pipe', 'fsdp'), may hold values from -0.125 to 0.125
- down_weight: bfloat16 [2, 7168, 2560], P('pipe', 'fsdp'), may hold values from -0.0625 to 0.0625
- router_in: bfloat16 [2, 2560, 256], P('pipe', 'fsdp'), may hold values from -0.125 to 0.125
- router_bias: float32 [2, 50, 256], P('pipe'), may hold values from -6 to 6
- router_out: float32 [2, 256], P('pipe'), may hold values from -0.375 to 0.375
- out_cotangent: bfloat16 [2, 1024, 2560], P('dp', 'fsdp'), may hold values from -0.119628906 to 0.119628906
Outputs:
- blended: bfloat16 [2, 2, 1024, 2560], P('pipe', 'dp', 'fsdp')
- grad_router_in: float32 [2, 2560, 256], P('pipe', 'fsdp')
- grad_router_bias: float32 [2, 50, 256], P('pipe')
- grad_router_out: float32 [2, 256], P('pipe')
Inputs may be any that keep to these rules, and one draw needn't show every extreme that they name: `fresh_mask`: for each section and video, the 128 consecutive tokens of one index of fsdp hold 1 to 2 ones, and some index holds exactly 2.
All inputs are finite; a program needn't handle non-finite values.
Results may differ from a plain program's by a relative error of at most 0.023.
Values may be sent and summed in bfloat16 or wider, within the bound.
A program may use at most 64 MiB of HBM per device.

v0:
```python
import jax
import jax.numpy as jnp
from jax import lax
from jax.sharding import PartitionSpec as P

FRESH = 2
layer_eps = 1e-06
gelu_scale = 0.7978845608028654
gelu_cubic = 0.044715


def from_behind(block, axis, distance):
    devices = range(lax.axis_size(axis))
    route = [(i - distance, i) for i in devices if i - distance in devices]
    return lax.ppermute(block, axis, route)


def for_sending(value):
    return jax.tree.map(lambda a: a.astype(jnp.bfloat16) if a.dtype == jnp.float32 else a, value)


def gelu_tanh(values):
    inner_arg = gelu_scale * (values + gelu_cubic * values * values * values)
    return 0.5 * values * (1.0 + jnp.tanh(inner_arg))


def gelu_slope(values):
    inner_arg = gelu_scale * (values + gelu_cubic * values * values * values)
    tanh_val = jnp.tanh(inner_arg)
    return 0.5 * (1.0 + tanh_val) + 0.5 * values * (1.0 - tanh_val * tanh_val) * gelu_scale * (
        1.0 + 3.0 * gelu_cubic * values * values
    )


def normalize(inputs):
    values = inputs.astype(jnp.float32)
    center = values - jnp.mean(values, axis=1, keepdims=True)
    inv_std = lax.rsqrt(jnp.mean(center * center, axis=1, keepdims=True) + layer_eps)
    return (center * inv_std, inv_std)


def normalize_back(scaled, inv_std, grads):
    return inv_std * (
        grads
        - jnp.mean(grads, axis=1, keepdims=True)
        - scaled * jnp.mean(grads * scaled, axis=1, keepdims=True)
    )


def contract_last(left, right):
    return lax.dot_general(
        left, right, (((1,), (1,)), ((), ())), preferred_element_type=jnp.float32
    )


def contract_first(left, right):
    return lax.dot_general(
        left, right, (((0,), (0,)), ((), ())), preferred_element_type=jnp.float32
    )


def gather_gate(gate_grad):
    return lax.all_gather(gate_grad, "fsdp", axis=0, tiled=True)


def body(
    video_tokens,
    cached_out,
    fresh_mask,
    timestep,
    up_weight,
    down_weight,
    router_in,
    router_bias,
    router_out,
    out_cotangent,
):
    section_id = lax.axis_index("pipe")
    column_slot = lax.axis_index("fsdp")
    inputs_first = video_tokens[0]
    cached = cached_out[0, 0]
    mask_row = fresh_mask[0, 0]
    w_up = up_weight[0]
    w_down = down_weight[0]
    r_in = router_in[0]
    r_out = router_out[0]
    tok_rows = inputs_first.shape[0]
    shard_cols = r_in.shape[0]
    hot_step = (jnp.arange(router_bias.shape[1]) == timestep[0]).astype(jnp.float32)
    bias_row = jnp.dot(hot_step, router_bias[0], precision=lax.Precision.HIGHEST)
    picked = jnp.argsort(1 - mask_row, stable=True)[:FRESH]
    live_rows = (jnp.arange(FRESH) < jnp.sum(mask_row)).astype(jnp.float32)

    def select(values):
        return jnp.take(values, picked, axis=0)

    def spread(values):
        return jnp.zeros((tok_rows, values.shape[1]), values.dtype).at[picked].add(values)

    def forward(inputs):
        rows_in = select(inputs)
        rows_cached = select(cached).astype(jnp.float32)
        scaled, inv_std = normalize(rows_in)
        normed = scaled.astype(jnp.bfloat16)
        row_count = normed.shape[0]
        gathered = lax.all_gather(normed, "fsdp", axis=0, tiled=True)
        pre_act = contract_last(gathered, w_up)
        hid_act = gelu_tanh(pre_act).astype(jnp.bfloat16)
        block_sum = lax.psum_scatter(
            jnp.dot(hid_act, w_down, preferred_element_type=jnp.float32).astype(jnp.bfloat16),
            "fsdp",
            scatter_dimension=0,
            tiled=True,
        ).astype(jnp.float32)
        columns = lax.dynamic_slice_in_dim(gathered, column_slot * shard_cols, shard_cols, 1)
        router_part = jnp.dot(columns, r_in, preferred_element_type=jnp.float32)
        router_pre = (
            lax.psum(router_part.astype(jnp.bfloat16), "fsdp").astype(jnp.float32)
            + bias_row[None, :]
        )
        gate_all = jax.nn.sigmoid(
            jnp.dot(gelu_tanh(router_pre), r_out, precision=lax.Precision.HIGHEST)
        )
        gate_own = lax.dynamic_slice_in_dim(gate_all, column_slot * row_count, row_count, 0)
        fresh_out = rows_in.astype(jnp.float32) + block_sum
        delta_rows = live_rows[:, None] * gate_own[:, None] * (fresh_out - rows_cached)
        blended = (cached.astype(jnp.float32) + spread(delta_rows)).astype(jnp.bfloat16)
        stored = (
            scaled,
            inv_std,
            columns,
            pre_act,
            router_pre,
            gate_all,
            gate_own,
            fresh_out,
            rows_cached,
        )
        return (blended, stored)

    def local_grads(stored, cot_rows):
        gate_own = stored[6]
        fresh_out = stored[7]
        rows_cached = stored[8]
        gate_grad = jnp.sum(cot_rows * live_rows[:, None] * (fresh_out - rows_cached), axis=1)
        fresh_grad = cot_rows * (live_rows * gate_own)[:, None]
        return (gate_grad, fresh_grad)

    def router_grads(stored, gate_all_grad):
        columns = stored[2]
        router_pre = stored[4]
        gate_all = stored[5]
        logit_grad = gate_all_grad * gate_all * (1.0 - gate_all)
        out_grad = jnp.dot(logit_grad, gelu_tanh(router_pre), precision=lax.Precision.HIGHEST)
        hidden_grad = logit_grad[:, None] * r_out[None, :] * gelu_slope(router_pre)
        hidden_b = hidden_grad.astype(jnp.bfloat16)
        in_grad = contract_first(columns, hidden_b)
        bias_grad = hot_step[:, None] * jnp.sum(hidden_grad, axis=0)[None, :]
        return (hidden_b, (in_grad, bias_grad, out_grad))

    blended_first, stored_first = forward(inputs_first)
    arriving = from_behind(blended_first, "pipe", 1)
    inputs_second = jnp.where(section_id == 1, arriving, inputs_first)
    blended_out, stored = forward(inputs_second)
    cot_second = select(out_cotangent[0]).astype(jnp.float32)
    gate_grad, fresh_grad = local_grads(stored, cot_second)
    hidden_b, grads_second = router_grads(stored, gather_gate(gate_grad))
    fresh_rows = lax.all_gather(fresh_grad.astype(jnp.bfloat16), "fsdp", axis=0, tiled=True)
    act_grad = contract_last(fresh_rows, w_down)
    pre_grad = (act_grad * gelu_slope(stored[3])).astype(jnp.bfloat16)
    row_count = fresh_grad.shape[0]
    total_rows = jnp.dot(pre_grad, w_up, preferred_element_type=jnp.float32)
    router_term = contract_last(hidden_b, r_in)
    current = lax.dynamic_slice_in_dim(total_rows, column_slot * shard_cols, shard_cols, 1)
    normed_grad = lax.psum_scatter(
        lax.dynamic_update_slice_in_dim(
            total_rows, current + router_term, column_slot * shard_cols, 1
        ).astype(jnp.bfloat16),
        "fsdp",
        scatter_dimension=0,
        tiled=True,
    ).astype(jnp.float32)
    input_grad = fresh_grad + normalize_back(stored[0], stored[1], normed_grad)
    positions = picked.astype(jnp.float32)
    got_rows, got_positions = from_behind((input_grad, positions), "pipe", -1)
    returning = (
        jnp.zeros((tok_rows, input_grad.shape[1]), jnp.float32)
        .at[got_positions.astype(jnp.int32)]
        .add(got_rows)
    )
    gate_grad_first, unused_grad = local_grads(stored, select(returning))
    unused_hidden, grads_first = router_grads(stored, gather_gate(gate_grad_first))
    chosen = tuple(
        (
            jnp.where(section_id == 1, second_grad, first_grad)
            for second_grad, first_grad in zip(grads_second, grads_first)
        )
    )
    summed = jax.tree.map(
        lambda part: part.astype(jnp.float32), lax.psum(for_sending(chosen), "dp")
    )
    return (blended_out[None, None], summed[0][None], summed[1][None], summed[2][None])


def solution(mesh):
    placed = (
        P("dp", "fsdp", None),
        P("pipe", "dp", "fsdp", None),
        P("pipe", "dp", "fsdp"),
        P("dp"),
        P("pipe", "fsdp", None),
        P("pipe", "fsdp", None),
        P("pipe", "fsdp", None),
        P("pipe", None, None),
        P("pipe", None),
        P("dp", "fsdp", None),
    )
    return jax.shard_map(
        body,
        mesh=mesh,
        in_specs=placed,
        out_specs=(
            P("pipe", "dp", "fsdp", None),
            P("pipe", "fsdp", None),
            P("pipe", None, None),
            P("pipe", None),
        ),
        check_vma=False,
    )
```

profile of v0, /device:TPU:0, one launch (start us, length us, event | category | flops | bytes accessed | tf_op | source)
XLA Modules:
  0.0 421.7 jit_solution(18369744704275985153)
XLA Ops:
  7.2 1.3 fusion.193
  8.6 2.5 sort.17
  11.1 1.8 gather_fusion.1
  12.9 0.2 convert_reduce_fusion.2
  13.1 0.2 fusion.87
  13.4 32.4 %all-gather = bf16[8,2,2560]{2,1,0:T(2,128)(2,1)S(1)} all-gather(bf16[1,2,2560]{2,1,0:T(2,128)(2,1)S(1)} %fusion.127), channel_id=1, replica_groups=mesh['fsdp'=8,'pipe'=2,'dp'=2] {'fsdp'}, dimensions={0}, use_global_device_ids=true | all-gather | bytes 92160 | tf_op jit(solution)/shard_map/all_gather | solution.py:106
  45.8 6.5 %fusion.12 = bf16[16,2560]{1,0:T(8,128)(2,1)} fusion(bf16[1,896,2560]{2,1,0:T(8,128)(2,1)} %param.17, bf16[16,2560]{1,0:T(8,128)(2,1)S(1)} %reshape.151, bf16[1,896,2560]{2,1,0:T(8,128)(2,1)} %param.16), kind=kOutput, calls=%fused_computation.20 | convolution fusion | flops 146970624 | bytes 9338880 | tf_op jit(solution)/shard_map/dot_general | solution.py:110
  52.5 0.2 convolution_convert_fusion.1
  52.7 21.6 %psum.35 = bf16[16,256]{1,0:T(8,128)(2,1)S(1)} all-reduce(bf16[16,256]{1,0:T(8,128)(2,1)S(1)} %convolution_convert_fusion.1), channel_id=1, replica_groups=mesh['fsdp'=8,'pipe'=2,'dp'=2] {'fsdp'}, use_global_device_ids=true, to_apply=%region_4.6 | all-reduce | flops 4096 | bytes 16384 | tf_op jit(solution)/shard_map/psum | solution.py:118
  74.9 0.1 bitcast_convert_fusion
  75.0 0.6 gather_fusion.2
  75.7 0.1 fusion.52
  75.9 0.6 fusion.192
  77.1 0.1 fusion.33
  77.3 0.7 dynamic-slice_select_fusion.1
  78.0 45.0 %all-reduce.13.cloned.1.call-done = bf16[16,2560]{1,0:T(8,128)(2,1)} async-done(((bf16[16,2560]{1,0:T(8,128)(2,1)}), bf16[16,2560]{1,0:T(8,128)(2,1)}) %all-reduce.13.cloned.1.call-update) | async-done | bytes 81936
  123.0 1.4 scatter_custom_fusion
  124.4 0.9 convert_element_type.120
  125.3 1.3 collective-permute-start
  126.7 1.3 collective-permute-start.1
  128.0 0.6 gather_fusion.4
  129.1 0.7 fusion.156
  129.8 1.2 broadcast_select_fusion
  131.0 0.6 gather_fusion.3
  131.6 0.2 convert_reduce_fusion.1
  131.8 0.2 fusion.86
  132.0 0.1 fusion.126
  132.1 30.5 %all-gather.1 = bf16[8,2,2560]{2,1,0:T(2,128)(2,1)S(1)} all-gather(bf16[1,2,2560]{2,1,0:T(2,128)(2,1)S(1)} %fusion.126), channel_id=1, replica_groups=mesh['fsdp'=8,'pipe'=2,'dp'=2] {'fsdp'}, dimensions={0}, use_global_device_ids=true | all-gather | bytes 92160 | tf_op jit(solution)/shard_map/all_gather | solution.py:106
  162.7 3.6 fusion.8
  166.3 0.2 convolution_convert_fusion
  166.5 3.7 fusion.15
  170.2 20.5 %psum.36 = bf16[16,256]{1,0:T(8,128)(2,1)S(1)} all-reduce(bf16[16,256]{1,0:T(8,128)(2,1)S(1)} %convolution_convert_fusion), channel_id=1, replica_groups=mesh['fsdp'=8,'pipe'=2,'dp'=2] {'fsdp'}, use_global_device_ids=true, to_apply=%region_9.11 | all-reduce | flops 4096 | bytes 16384 | tf_op jit(solution)/shard_map/psum | solution.py:118
  190.7 0.1 fusion.31
  190.8 0.7 dynamic-slice_select_fusion
  191.6 48.1 %all-reduce.15.cloned.1.call-done = bf16[16,2560]{1,0:T(8,128)(2,1)} async-done(((bf16[16,2560]{1,0:T(8,128)(2,1)}), bf16[16,2560]{1,0:T(8,128)(2,1)}) %all-reduce.15.cloned.1.call-update) | async-done | bytes 81936
  239.6 1.0 fusion.93
  240.6 30.5 %all-gather.2 = bf16[8,2,2560]{2,1,0:T(2,128)(2,1)S(1)} all-gather(bf16[1,2,2560]{2,1,0:T(2,128)(2,1)S(1)} %get-tuple-element.21), channel_id=1, replica_groups=mesh['fsdp'=8,'pipe'=2,'dp'=2] {'fsdp'}, dimensions={0}, use_global_device_ids=true | all-gather | bytes 92160 | tf_op jit(solution)/shard_map/all_gather | solution.py:168
  271.2 0.2 dynamic-update-slice
  271.5 5.8 %fusion.6 = f32[16,2560]{1,0:T(8,128)S(1)} fusion(bf16[1,896,2560]{2,1,0:T(8,128)(2,1)} %param.16, bf16[16,2560]{1,0:T(8,128)(2,1)S(1)} %reshape.155, bf16[1,896,2560]{2,1,0:T(8,128)(2,1)} %param.17, f32[16,896]{1,0:T(8,128)S(1)} %fusion.8), kind=kOutput, calls=%fused_computation.14 | convolution fusion | flops 147073024 | bytes 9478144 | tf_op jit(solution)/shard_map/dot_general | solution.py:172
  277.3 20.1 %all-reduce = f32[16]{0:T(128)S(1)} all-reduce(f32[16]{0:T(128)S(1)} %dynamic-update-slice), channel_id=1, replica_groups=mesh['fsdp'=8,'pipe'=2,'dp'=2] {'fsdp'}, use_global_device_ids=true, to_apply=%add | all-reduce | flops 16 | bytes 128
  297.4 0.2 convolution_add_fusion
  297.6 0.4 dynamic_update_slice.3
  298.0 0.6 convert_element_type.136
  298.7 1.2 scatter_custom_fusion.1
  299.9 0.9 convert_bitcast_fusion
  300.8 64.7 %all-reduce.17.cloned.1.call-done = bf16[16,2560]{1,0:T(8,128)(2,1)} async-done(((bf16[16,2560]{1,0:T(8,128)(2,1)}), bf16[16,2560]{1,0:T(8,128)(2,1)}) %all-reduce.17.cloned.1.call-update) | async-done | bytes 81936
  365.6 1.0 convert_reduce_fusion
  366.6 0.9 fusion.80
  367.5 1.3 collective-permute-start.2
  368.8 0.3 fusion.129
  369.1 1.5 collective-permute-done.2
  370.5 1.0 scatter_custom_fusion.2
  371.5 0.6 gather_fusion
  372.1 0.2 multiply_reduce_fusion
  372.3 0.2 dynamic-update-slice.1
  372.5 0.1 fusion.142
  372.7 20.2 %all-reduce.1 = f32[16]{0:T(128)S(1)} all-reduce(f32[16]{0:T(128)S(1)} %dynamic-update-slice.1), channel_id=1, replica_groups=mesh['fsdp'=8,'pipe'=2,'dp'=2] {'fsdp'}, use_global_device_ids=true, to_apply=%add.1 | all-reduce | flops 16 | bytes 128
  392.8 0.2 fusion.140
  393.1 1.0 fusion.19
  394.2 8.9 %all-reduce.5 = (bf16[1,50,256]{2,0,1:T(2,128)(2,1)S(1)}, bf16[1,256]{1,0:T(2,128)(2,1)S(1)}) all-reduce(bf16[1,50,256]{2,0,1:T(2,128)(2,1)S(1)} %broadcast_in_dim.75, bf16[1,256]{1,0:T(2,128)(2,1)S(1)} %broadcast_in_dim.77), channel_id=1, replica_groups=mesh['fsdp'=8,'pipe'=2,'dp'=2] {'dp'}, use_global_device_ids=true, to_apply=%region_21.23 | all-reduce | flops 13056 | bytes 52224 | tf_op jit(solution)/shard_map/psum | solution.py:200
  403.1 0.7 broadcast_in_dim.76
  403.8 0.6 broadcast_in_dim.78
  404.4 9.1 %all-reduce.11.cloned.1.call-done = bf16[1,320,256]{2,1,0:T(8,128)(2,1)} async-done(((bf16[1,320,256]{2,1,0:T(8,128)(2,1)}), bf16[1,320,256]{2,1,0:T(8,128)(2,1)}) %all-reduce.11.cloned.1.call-update) | async-done | bytes 163856 | tf_op jit(solution)/shard_map/psum | solution.py:200
  413.5 1.7 broadcast_in_dim.74
  (47 shorter events, 0.8 us)
Async XLA Ops:
  7.2 120.8 %copy-start = (bf16[1,128,2560]{2,1,0:T(8,128)(2,1)S(1)}, bf16[1,128,2560]{2,1,0:T(8,128)(2,1)}, u32[]{:S(2)}) copy-start(bf16[1,128,2560]{2,1,0:T(8,128)(2,1)} %param.21) | copy-start | bytes 1966084
  7.2 115.8 %all-reduce.13.cloned.1.call-start = ((), (), s32[]{:S(2)}) async-start(), calls=%async_computation.1 | async-start | bytes 163840
  45.8 6.6 %copy-start.1 = (bf16[1,320,256]{2,1,0:T(8,128)(2,1)S(1)}, bf16[1,320,256]{2,1,0:T(8,128)(2,1)}, u32[]{:S(2)}) copy-start(bf16[1,320,256]{2,1,0:T(8,128)(2,1)} %param.18) | copy-start | bytes 491524
  45.8 29.1 %copy-start.2 = (bf16[1,1,128,2560]{3,2,1,0:T(8,128)(2,1)S(1)}, bf16[1,1,128,2560]{3,2,1,0:T(8,128)(2,1)}, u32[]{:S(2)}) copy-start(bf16[1,1,128,2560]{3,2,1,0:T(8,128)(2,1)} %param.13) | copy-start | bytes 1966084
  52.3 23.4 %copy-start.3 = (f32[1,50,256]{2,0,1:T(1,128)S(1)}, f32[1,50,256]{2,0,1:T(1,128)}, u32[]{:S(2)}) copy-start(f32[1,50,256]{2,0,1:T(1,128)} %param.19) | copy-start | bytes 153604
  52.4 23.5 %copy-start.5 = (u32[32]{0:T(128)S(1)}, u32[32]{0:T(128)}, u32[]{:S(2)}) copy-start(u32[32]{0:T(128)} %constant.94) | copy-start | bytes 388
  52.4 24.8 %copy-start.4 = (f32[1,256]{1,0:T(1,128)S(1)}, f32[1,256]{1,0:T(1,128)}, u32[]{:S(2)}) copy-start(f32[1,256]{1,0:T(1,128)} %param.20) | copy-start | bytes 3076
  52.4 187.3 %all-reduce.15.cloned.1.call-start = ((), (), s32[]{:S(2)}) async-start(), calls=%async_computation.2 | async-start | bytes 163840
  125.3 4.5 %collective-permute-start = (bf16[128,2560]{1,0:T(8,128)(2,1)}, bf16[128,2560]{1,0:T(8,128)(2,1)S(1)}, u32[]{:S(2)}, u32[]{:S(2)}) collective-permute-start(bf16[128,2560]{1,0:T(8,128)(2,1)} %convert_element_type.120), channel_id=1, source_target_pairs={{0,2},{1,3},{4,6},{5,7},{8,10},{9,11},{12,14},{13,15},{16,18},{17,... | collective-permute-start | bytes 1966088 | tf_op jit(solution)/shard_map/ppermute | solution.py:15
  126.7 3.1 collective-permute-start.1
  170.2 195.4 %all-reduce.17.cloned.1.call-start = ((), (), s32[]{:S(2)}) async-start(), calls=%async_computation.3 | async-start | bytes 163840
  298.6 114.8 %all-reduce.11.cloned.1.call-start = ((), (), s32[]{:S(2)}) async-start(), calls=%async_computation | async-start | bytes 327680 | tf_op jit(solution)/shard_map/psum | solution.py:200
  367.5 3.1 collective-permute-start.2
Sparse Core Ops, SparseCore 0:
  52.5 70.4 all-reduce.12
  170.3 69.3 all-reduce.14
  298.8 66.7 all-reduce.16
  394.2 19.2 all-reduce.10
where the time goes:
time: 422 us
  blocking collectives  185 us (44%)
  waiting for transfers between devices  168 us (40%)
  matrix products  22.2 us (5%)
  other arithmetic  20.6 us (5%)
  between operations  16 us (4%)
  local copies, waits for them, and re-layouts  5.75 us (1%)
    unnamed x7, waiting for transfers between devices  158 us
    all_gather x2, blocking collectives, forward(): gathered = lax.all_gather(normed, 'fsdp', axis=0, tiled=True)  62.9 us
    psum x2, blocking collectives, forward(): lax.psum(router_part.astype(jnp.bfloat16), 'fsdp').astype(jnp.float32)  42.1 us
    unnamed x2, blocking collectives  40.3 us
    all_gather x1, blocking collectives, body(): lax.all_gather(fresh_grad.astype(jnp.bfloat16), 'fsdp', axis=0, tiled=True)  30.5 us
    dot_general x2, matrix products, forward(): jnp.dot(hid_act, w_down, preferred_element_type=jnp.float32)  10.2 us
    psum x1, waiting for transfers between devices, body(): lax.psum(for_sending(chosen), 'dp')  9.1 us
    psum x1, blocking collectives, body(): lax.psum(for_sending(chosen), 'dp')  8.92 us
  transfers between devices with their start and end apart: 7, of which 5 were waited for; matrix products, arithmetic and copies ran while one was open for 2% of the time, Pallas kernels for 0%

commit v1 on v0

--- a/solution.py
+++ b/solution.py
@@ -103,7 +103,14 @@
         scaled, inv_std = normalize(rows_in)
         normed = scaled.astype(jnp.bfloat16)
         row_count = normed.shape[0]
-        gathered = lax.all_gather(normed, "fsdp", axis=0, tiled=True)
+        ring = [normed]
+        for hop in range(7):
+            ring.append(lax.ppermute(ring[-1], "fsdp", [(dev, (dev + 1) % 8) for dev in range(8)]))
+        gathered = jnp.roll(
+            jnp.concatenate(ring[::-1], axis=0),
+            (lax.axis_index("fsdp") + 1) * ring[0].shape[0],
+            axis=0,
+        )
         pre_act = contract_last(gathered, w_up)
         hid_act = gelu_tanh(pre_act).astype(jnp.bfloat16)
         block_sum = lax.psum_scatter(

time: 422 us -> 467 us (1.11)
  waiting for transfers between devices: 168 us -> 268 us
  blocking collectives: 185 us -> 118 us
    ppermute x0 -> x14, waiting for transfers between devices: none -> 75.8 us  [forward(): lax.ppermute(ring[-1], 'fsdp', [(dev, (dev + 1) % 8) for dev in range(8)])]
    all_gather x2 -> x0, blocking collectives: 62.9 us -> none  [forward(): gathered = lax.all_gather(normed, 'fsdp', axis=0, tiled=True)]
    unnamed x7, waiting for transfers between devices: 158 us -> 181 us
  transfers between devices with their start and end apart: 7 -> 21, of which waited for: 5 -> 20; matrix products, arithmetic and copies ran while one was open for 2% -> 6% of each run, Pallas kernels for 0% -> 0%
where the time goes in v1:
time: 467 us; the launch traced here: 466 us
  waiting for transfers between devices  268 us (57%)
  blocking collectives  118 us (25%)
  matrix products  24.4 us (5%)
  other arithmetic  22.8 us (5%)
  between operations  16.1 us (3%)
  starting transfers between devices  8.38 us (2%)
  local copies, waits for them, and re-layouts  8.02 us (2%)
    unnamed x7, waiting for transfers between devices  181 us
    ppermute x14, waiting for transfers between devices, forward(): lax.ppermute(ring[-1], 'fsdp', [(dev, (dev + 1) % 8) for dev in range(8)])  75.8 us
    unnamed x2, blocking collectives  40.3 us
    psum x2, blocking collectives, forward(): lax.psum(router_part.astype(jnp.bfloat16), 'fsdp').astype(jnp.float32)  37.9 us
    all_gather x1, blocking collectives, body(): lax.all_gather(fresh_grad.astype(jnp.bfloat16), 'fsdp', axis=0, tiled=True)  30.5 us
    dot_general x2, matrix products, forward(): jnp.dot(hid_act, w_down, preferred_element_type=jnp.float32)  10.2 us
  transfers between devices with their start and end apart: 21, of which 20 were waited for; matrix products, arithmetic and copies ran while one was open for 6% of the time, Pallas kernels for 0%

profile of v1, /device:TPU:0, one launch (start us, length us, event | category | flops | bytes accessed | tf_op | source)
XLA Modules:
  0.0 465.6 jit_solution(680879602119435941)
XLA Ops:
  7.2 1.3 fusion.204
  8.6 2.5 sort.17
  11.6 1.8 gather_fusion.1
  13.9 3.0 collective-permute-start
  16.9 4.7 %collective-permute-done = bf16[2,2560]{1,0:T(2,128)(2,1)S(1)} collective-permute-done((bf16[2,2560]{1,0:T(2,128)(2,1)S(1)}, bf16[2,2560]{1,0:T(2,128)(2,1)S(1)}, u32[]{:S(2)}, u32[]{:S(2)}) %collective-permute-start) | collective-permute-done | bytes 10272 | tf_op jit(solution)/shard_map/ppermute | solution.py:108
  21.6 6.4 %collective-permute-done.1 = bf16[2,2560]{1,0:T(2,128)(2,1)S(1)} collective-permute-done((bf16[2,2560]{1,0:T(2,128)(2,1)S(1)}, bf16[2,2560]{1,0:T(2,128)(2,1)S(1)}, u32[]{:S(2)}, u32[]{:S(2)}) %collective-permute-start.1) | collective-permute-done | bytes 10272 | tf_op jit(solution)/shard_map/ppermute | solution.py:108
  28.0 6.4 %collective-permute-done.2 = bf16[2,2560]{1,0:T(2,128)(2,1)S(1)} collective-permute-done((bf16[2,2560]{1,0:T(2,128)(2,1)S(1)}, bf16[2,2560]{1,0:T(2,128)(2,1)S(1)}, u32[]{:S(2)}, u32[]{:S(2)}) %collective-permute-start.2) | collective-permute-done | bytes 10272 | tf_op jit(solution)/shard_map/ppermute | solution.py:108
  34.4 6.4 %collective-permute-done.3 = bf16[2,2560]{1,0:T(2,128)(2,1)S(1)} collective-permute-done((bf16[2,2560]{1,0:T(2,128)(2,1)S(1)}, bf16[2,2560]{1,0:T(2,128)(2,1)S(1)}, u32[]{:S(2)}, u32[]{:S(2)}) %collective-permute-start.3) | collective-permute-done | bytes 10272 | tf_op jit(solution)/shard_map/ppermute | solution.py:108
  40.7 6.4 %collective-permute-done.4 = bf16[2,2560]{1,0:T(2,128)(2,1)S(1)} collective-permute-done((bf16[2,2560]{1,0:T(2,128)(2,1)S(1)}, bf16[2,2560]{1,0:T(2,128)(2,1)S(1)}, u32[]{:S(2)}, u32[]{:S(2)}) %collective-permute-start.4) | collective-permute-done | bytes 10272 | tf_op jit(solution)/shard_map/ppermute | solution.py:108
  47.1 1.2 bitcast_convert_fusion
  49.0 4.5 collective-permute-done.5
  53.5 1.5 fusion.56
  55.0 1.7 gather_fusion.2
  56.9 0.7 fusion.203
  58.2 1.7 collective-permute-done.6
  60.0 6.5 %fusion.12 = bf16[16,2560]{1,0:T(8,128)(2,1)} fusion(bf16[1,896,2560]{2,1,0:T(8,128)(2,1)} %param.19, bf16[1,896,2560]{2,1,0:T(8,128)(2,1)} %param.18, s32[]{:T(128)S(6)} %select_n.96, bf16[16,2560]{1,0:T(8,128)(2,1)S(1)} %concatenate.9), kind=kOutput, calls=%fused_computation.20 | convolution fusion | flops 147134464 | bytes 9338884 | tf_op jit(solution)/shard_map/dot_general | solution.py:117
  66.8 20.5 %psum.35 = bf16[16,256]{1,0:T(8,128)(2,1)S(1)} all-reduce(bf16[16,256]{1,0:T(8,128)(2,1)S(1)} %convolution_convert_fusion.1), channel_id=1, replica_groups=mesh['fsdp'=8,'pipe'=2,'dp'=2] {'fsdp'}, use_global_device_ids=true, to_apply=%region_4.7 | all-reduce | flops 4096 | bytes 16384 | tf_op jit(solution)/shard_map/psum | solution.py:125
  87.3 0.8 fusion.33
  88.1 0.7 dynamic-slice_select_fusion.1
  88.8 47.3 %all-reduce.13.cloned.1.call-done = bf16[16,2560]{1,0:T(8,128)(2,1)} async-done(((bf16[16,2560]{1,0:T(8,128)(2,1)}), bf16[16,2560]{1,0:T(8,128)(2,1)}) %all-reduce.13.cloned.1.call-update) | async-done | bytes 81936
  136.2 1.4 scatter_custom_fusion
  137.6 0.9 convert_element_type.120
  138.5 1.3 collective-permute-start.7
  139.9 1.9 collective-permute-done.7
  141.7 1.2 broadcast_select_fusion
  142.9 0.7 gather_fusion.3
  143.6 0.9 convert_reduce_fusion.1
  144.8 1.3 collective-permute-start.8
  146.1 5.1 %collective-permute-done.8 = bf16[2,2560]{1,0:T(2,128)(2,1)S(1)} collective-permute-done((bf16[2,2560]{1,0:T(2,128)(2,1)S(1)}, bf16[2,2560]{1,0:T(2,128)(2,1)S(1)}, u32[]{:S(2)}, u32[]{:S(2)}) %collective-permute-start.8) | collective-permute-done | bytes 10272 | tf_op jit(solution)/shard_map/ppermute | solution.py:108
  151.2 6.4 %collective-permute-done.9 = bf16[2,2560]{1,0:T(2,128)(2,1)S(1)} collective-permute-done((bf16[2,2560]{1,0:T(2,128)(2,1)S(1)}, bf16[2,2560]{1,0:T(2,128)(2,1)S(1)}, u32[]{:S(2)}, u32[]{:S(2)}) %collective-permute-start.9) | collective-permute-done | bytes 10272 | tf_op jit(solution)/shard_map/ppermute | solution.py:108
  157.6 6.4 %collective-permute-done.10 = bf16[2,2560]{1,0:T(2,128)(2,1)S(1)} collective-permute-done((bf16[2,2560]{1,0:T(2,128)(2,1)S(1)}, bf16[2,2560]{1,0:T(2,128)(2,1)S(1)}, u32[]{:S(2)}, u32[]{:S(2)}) %collective-permute-start.10) | collective-permute-done | bytes 10272 | tf_op jit(solution)/shard_map/ppermute | solution.py:108
  164.0 6.4 %collective-permute-done.11 = bf16[2,2560]{1,0:T(2,128)(2,1)S(1)} collective-permute-done((bf16[2,2560]{1,0:T(2,128)(2,1)S(1)}, bf16[2,2560]{1,0:T(2,128)(2,1)S(1)}, u32[]{:S(2)}, u32[]{:S(2)}) %collective-permute-start.11) | collective-permute-done | bytes 10272 | tf_op jit(solution)/shard_map/ppermute | solution.py:108
  170.3 0.6 slice_convert_fusion
  170.9 1.3 collective-permute-start.15
  172.2 4.5 collective-permute-done.12
  177.3 5.8 %collective-permute-done.13 = bf16[2,2560]{1,0:T(2,128)(2,1)S(1)} collective-permute-done((bf16[2,2560]{1,0:T(2,128)(2,1)S(1)}, bf16[2,2560]{1,0:T(2,128)(2,1)S(1)}, u32[]{:S(2)}, u32[]{:S(2)}) %collective-permute-start.13) | collective-permute-done | bytes 10272 | tf_op jit(solution)/shard_map/ppermute | solution.py:108
  183.1 0.7 gather_fusion.4
  184.5 5.0 %collective-permute-done.14 = bf16[2,2560]{1,0:T(2,128)(2,1)S(1)} collective-permute-done((bf16[2,2560]{1,0:T(2,128)(2,1)S(1)}, bf16[2,2560]{1,0:T(2,128)(2,1)S(1)}, u32[]{:S(2)}, u32[]{:S(2)}) %collective-permute-start.14) | collective-permute-done | bytes 10272 | tf_op jit(solution)/shard_map/ppermute | solution.py:108
  189.8 3.6 fusion.8
  193.4 17.4 %psum.36 = bf16[16,256]{1,0:T(8,128)(2,1)S(1)} all-reduce(bf16[16,256]{1,0:T(8,128)(2,1)S(1)} %convolution_convert_fusion), channel_id=1, replica_groups=mesh['fsdp'=8,'pipe'=2,'dp'=2] {'fsdp'}, use_global_device_ids=true, to_apply=%region_9.12 | all-reduce | flops 4096 | bytes 16384 | tf_op jit(solution)/shard_map/psum | solution.py:125
  211.0 3.7 fusion.15
  214.7 0.6 dynamic-slice_select_fusion
  215.4 67.7 %all-reduce.15.cloned.1.call-done = bf16[16,2560]{1,0:T(8,128)(2,1)} async-done(((bf16[16,2560]{1,0:T(8,128)(2,1)}), bf16[16,2560]{1,0:T(8,128)(2,1)}) %all-reduce.15.cloned.1.call-update) | async-done | bytes 81936
  283.1 1.0 fusion.101
  284.3 20.1 %all-reduce = f32[16]{0:T(128)S(1)} all-reduce(f32[16]{0:T(128)S(1)} %dynamic-update-slice), channel_id=1, replica_groups=mesh['fsdp'=8,'pipe'=2,'dp'=2] {'fsdp'}, use_global_device_ids=true, to_apply=%add | all-reduce | flops 16 | bytes 128
  304.5 30.5 %all-gather = bf16[8,2,2560]{2,1,0:T(2,128)(2,1)S(1)} all-gather(bf16[1,2,2560]{2,1,0:T(2,128)(2,1)S(1)} %get-tuple-element.22), channel_id=1, replica_groups=mesh['fsdp'=8,'pipe'=2,'dp'=2] {'fsdp'}, dimensions={0}, use_global_device_ids=true | all-gather | bytes 92160 | tf_op jit(solution)/shard_map/all_gather | solution.py:175
  335.0 5.8 %fusion.6 = f32[16,2560]{1,0:T(8,128)S(1)} fusion(bf16[1,896,2560]{2,1,0:T(8,128)(2,1)} %param.18, bf16[16,2560]{1,0:T(8,128)(2,1)S(1)} %reshape.151, bf16[1,896,2560]{2,1,0:T(8,128)(2,1)} %param.19, f32[16,896]{1,0:T(8,128)S(1)} %fusion.8), kind=kOutput, calls=%fused_computation.14 | convolution fusion | flops 147073024 | bytes 9478144 | tf_op jit(solution)/shard_map/dot_general | solution.py:179
  341.4 0.6 convert_element_type.136
  342.1 1.3 scatter_custom_fusion.1
  343.5 65.5 %all-reduce.17.cloned.1.call-done = bf16[16,2560]{1,0:T(8,128)(2,1)} async-done(((bf16[16,2560]{1,0:T(8,128)(2,1)}), bf16[16,2560]{1,0:T(8,128)(2,1)}) %all-reduce.17.cloned.1.call-update) | async-done | bytes 81936
  409.0 1.0 convert_reduce_fusion
  410.0 0.9 fusion.88
  410.9 1.3 collective-permute-start.16
  412.2 0.9 convert_bitcast_fusion
  413.1 0.9 collective-permute-done.16
  414.0 1.0 scatter_custom_fusion.2
  414.9 0.7 gather_fusion
  416.2 20.2 %all-reduce.1 = f32[16]{0:T(128)S(1)} all-reduce(f32[16]{0:T(128)S(1)} %dynamic-update-slice.1), channel_id=1, replica_groups=mesh['fsdp'=8,'pipe'=2,'dp'=2] {'fsdp'}, use_global_device_ids=true, to_apply=%add.1 | all-reduce | flops 16 | bytes 128
  437.0 1.0 fusion.19
  438.1 8.9 %all-reduce.5 = (bf16[1,50,256]{2,0,1:T(2,128)(2,1)S(1)}, bf16[1,256]{1,0:T(2,128)(2,1)S(1)}) all-reduce(bf16[1,50,256]{2,0,1:T(2,128)(2,1)S(1)} %broadcast_in_dim.75, bf16[1,256]{1,0:T(2,128)(2,1)S(1)} %broadcast_in_dim.77), channel_id=1, replica_groups=mesh['fsdp'=8,'pipe'=2,'dp'=2] {'dp'}, use_global_device_ids=true, to_apply=%region_21.24 | all-reduce | flops 13056 | bytes 52224 | tf_op jit(solution)/shard_map/psum | solution.py:207
  447.1 0.7 broadcast_in_dim.76
  447.7 0.6 broadcast_in_dim.78
  448.3 9.1 %all-reduce.11.cloned.1.call-done = bf16[1,320,256]{2,1,0:T(8,128)(2,1)} async-done(((bf16[1,320,256]{2,1,0:T(8,128)(2,1)}), bf16[1,320,256]{2,1,0:T(8,128)(2,1)}) %all-reduce.11.cloned.1.call-update) | async-done | bytes 163856 | tf_op jit(solution)/shard_map/psum | solution.py:207
  457.4 1.7 broadcast_in_dim.74
  (81 shorter events, 5.3 us)
Async XLA Ops:
  7.2 175.9 %copy-start = (bf16[1,128,2560]{2,1,0:T(8,128)(2,1)S(1)}, bf16[1,128,2560]{2,1,0:T(8,128)(2,1)}, u32[]{:S(2)}) copy-start(bf16[1,128,2560]{2,1,0:T(8,128)(2,1)} %param.23) | copy-start | bytes 1966084
  7.2 49.7 %copy-start.7 = (u32[32]{0:T(128)S(1)}, u32[32]{0:T(128)}, u32[]{:S(2)}) copy-start(u32[32]{0:T(128)} %constant.111) | copy-start | bytes 388
  7.2 129.0 %all-reduce.13.cloned.1.call-start = ((), (), s32[]{:S(2)}) async-start(), calls=%async_computation.1 | async-start | bytes 163840
  11.1 0.5 copy-start.9
  11.1 45.6 %copy-start.3 = (pred[2]{0:T(512)(128)(4,1)}, pred[2]{0:T(512)(128)(4,1)S(1)}, u32[]{:S(2)}) copy-start(pred[2]{0:T(512)(128)(4,1)S(1)} %get-tuple-element.20) | copy-start | bytes 10
  11.1 48.7 %copy-start.8 = (s32[2]{0:T(128)}, s32[2]{0:T(128)S(1)}, u32[]{:S(2)}) copy-start(s32[2]{0:T(128)S(1)} %get-tuple-element.21) | copy-start | bytes 28
  11.6 46.5 %copy-start.6 = (s32[1024]{0:T(1024)}, s32[1024]{0:T(1024)S(1)}, u32[]{:S(2)}) copy-start(s32[1024]{0:T(1024)S(1)} %pad_clamp_fusion) | copy-start | bytes 12292
  13.9 7.7 %collective-permute-start = (bf16[2,2560]{1,0:T(2,128)(2,1)S(1)}, bf16[2,2560]{1,0:T(2,128)(2,1)S(1)}, u32[]{:S(2)}, u32[]{:S(2)}) collective-permute-start(bf16[2,2560]{1,0:T(2,128)(2,1)S(1)} %fusion.96), channel_id=1, source_target_pairs={{0,4},{4,8},{8,12},{12,16},{16,20},{20,24},{24,28},{28,0},{1,5},{5... | collective-permute-start | bytes 30728 | tf_op jit(solution)/shard_map/ppermute | solution.py:108
  21.6 6.4 %collective-permute-start.1 = (bf16[2,2560]{1,0:T(2,128)(2,1)S(1)}, bf16[2,2560]{1,0:T(2,128)(2,1)S(1)}, u32[]{:S(2)}, u32[]{:S(2)}) collective-permute-start(bf16[2,2560]{1,0:T(2,128)(2,1)S(1)} %collective-permute-done), channel_id=1, source_target_pairs={{0,4},{4,8},{8,12},{12,16},{16,20},{20,24},{24,28},{28,0},{1,5},{5... | collective-permute-start | bytes 30728 | tf_op jit(solution)/shard_map/ppermute | solution.py:108
  28.0 6.4 %collective-permute-start.2 = (bf16[2,2560]{1,0:T(2,128)(2,1)S(1)}, bf16[2,2560]{1,0:T(2,128)(2,1)S(1)}, u32[]{:S(2)}, u32[]{:S(2)}) collective-permute-start(bf16[2,2560]{1,0:T(2,128)(2,1)S(1)} %collective-permute-done.1), channel_id=1, source_target_pairs={{0,4},{4,8},{8,12},{12,16},{16,20},{20,24},{24,28},{28,0},{1,5},{5... | collective-permute-start | bytes 30728 | tf_op jit(solution)/shard_map/ppermute | solution.py:108
  34.4 6.4 %collective-permute-start.3 = (bf16[2,2560]{1,0:T(2,128)(2,1)S(1)}, bf16[2,2560]{1,0:T(2,128)(2,1)S(1)}, u32[]{:S(2)}, u32[]{:S(2)}) collective-permute-start(bf16[2,2560]{1,0:T(2,128)(2,1)S(1)} %collective-permute-done.2), channel_id=1, source_target_pairs={{0,4},{4,8},{8,12},{12,16},{16,20},{20,24},{24,28},{28,0},{1,5},{5... | collective-permute-start | bytes 30728 | tf_op jit(solution)/shard_map/ppermute | solution.py:108
  40.7 6.4 %collective-permute-start.4 = (bf16[2,2560]{1,0:T(2,128)(2,1)S(1)}, bf16[2,2560]{1,0:T(2,128)(2,1)S(1)}, u32[]{:S(2)}, u32[]{:S(2)}) collective-permute-start(bf16[2,2560]{1,0:T(2,128)(2,1)S(1)} %collective-permute-done.3), channel_id=1, source_target_pairs={{0,4},{4,8},{8,12},{12,16},{16,20},{20,24},{24,28},{28,0},{1,5},{5... | collective-permute-start | bytes 30728 | tf_op jit(solution)/shard_map/ppermute | solution.py:108
  47.1 6.4 %collective-permute-start.5 = (bf16[2,2560]{1,0:T(2,128)(2,1)S(1)}, bf16[2,2560]{1,0:T(2,128)(2,1)S(1)}, u32[]{:S(2)}, u32[]{:S(2)}) collective-permute-start(bf16[2,2560]{1,0:T(2,128)(2,1)S(1)} %collective-permute-done.4), channel_id=1, source_target_pairs={{0,4},{4,8},{8,12},{12,16},{16,20},{20,24},{24,28},{28,0},{1,5},{5... | collective-permute-start | bytes 30728 | tf_op jit(solution)/shard_map/ppermute | solution.py:108
  53.5 6.4 %collective-permute-start.6 = (bf16[2,2560]{1,0:T(2,128)(2,1)S(1)}, bf16[2,2560]{1,0:T(2,128)(2,1)S(1)}, u32[]{:S(2)}, u32[]{:S(2)}) collective-permute-start(bf16[2,2560]{1,0:T(2,128)(2,1)S(1)} %collective-permute-done.5), channel_id=1, source_target_pairs={{0,4},{4,8},{8,12},{12,16},{16,20},{20,24},{24,28},{28,0},{1,5},{5... | collective-permute-start | bytes 30728 | tf_op jit(solution)/shard_map/ppermute | solution.py:108
  60.0 6.6 %copy-start.1 = (bf16[1,320,256]{2,1,0:T(8,128)(2,1)S(1)}, bf16[1,320,256]{2,1,0:T(8,128)(2,1)}, u32[]{:S(2)}) copy-start(bf16[1,320,256]{2,1,0:T(8,128)(2,1)} %param.20) | copy-start | bytes 491524
  66.5 216.6 %all-reduce.15.cloned.1.call-start = ((), (), s32[]{:S(2)}) async-start(), calls=%async_computation.2 | async-start | bytes 163840
  137.6 73.2 %copy-start.2 = (f32[1,256]{1,0:T(1,128)S(1)}, f32[1,256]{1,0:T(1,128)}, u32[]{:S(2)}) copy-start(f32[1,256]{1,0:T(1,128)} %fusion.56) | copy-start | bytes 3076
  137.6 73.2 %copy-start.5 = (f32[1,256]{1,0:T(1,128)S(1)}, f32[1,256]{1,0:T(1,128)}, u32[]{:S(2)}) copy-start(f32[1,256]{1,0:T(1,128)} %param.22) | copy-start | bytes 3076
  138.5 3.2 collective-permute-start.7
  144.8 6.4 %collective-permute-start.8 = (bf16[2,2560]{1,0:T(2,128)(2,1)S(1)}, bf16[2,2560]{1,0:T(2,128)(2,1)S(1)}, u32[]{:S(2)}, u32[]{:S(2)}) collective-permute-start(bf16[2,2560]{1,0:T(2,128)(2,1)S(1)} %fusion.131), channel_id=1, source_target_pairs={{0,4},{4,8},{8,12},{12,16},{16,20},{20,24},{24,28},{28,0},{1,5},{5... | collective-permute-start | bytes 30728 | tf_op jit(solution)/shard_map/ppermute | solution.py:108
  151.2 6.4 %collective-permute-start.9 = (bf16[2,2560]{1,0:T(2,128)(2,1)S(1)}, bf16[2,2560]{1,0:T(2,128)(2,1)S(1)}, u32[]{:S(2)}, u32[]{:S(2)}) collective-permute-start(bf16[2,2560]{1,0:T(2,128)(2,1)S(1)} %collective-permute-done.8), channel_id=1, source_target_pairs={{0,4},{4,8},{8,12},{12,16},{16,20},{20,24},{24,28},{28,0},{1,5},{5... | collective-permute-start | bytes 30728 | tf_op jit(solution)/shard_map/ppermute | solution.py:108
  157.6 6.4 %collective-permute-start.10 = (bf16[2,2560]{1,0:T(2,128)(2,1)S(1)}, bf16[2,2560]{1,0:T(2,128)(2,1)S(1)}, u32[]{:S(2)}, u32[]{:S(2)}) collective-permute-start(bf16[2,2560]{1,0:T(2,128)(2,1)S(1)} %collective-permute-done.9), channel_id=1, source_target_pairs={{0,4},{4,8},{8,12},{12,16},{16,20},{20,24},{24,28},{28,0},{1,5},{5... | collective-permute-start | bytes 30728 | tf_op jit(solution)/shard_map/ppermute | solution.py:108
  164.0 6.4 %collective-permute-start.11 = (bf16[2,2560]{1,0:T(2,128)(2,1)S(1)}, bf16[2,2560]{1,0:T(2,128)(2,1)S(1)}, u32[]{:S(2)}, u32[]{:S(2)}) collective-permute-start(bf16[2,2560]{1,0:T(2,128)(2,1)S(1)} %collective-permute-done.10), channel_id=1, source_target_pairs={{0,4},{4,8},{8,12},{12,16},{16,20},{20,24},{24,28},{28,0},{1,5},{5... | collective-permute-start | bytes 30728 | tf_op jit(solution)/shard_map/ppermute | solution.py:108
  170.3 6.4 %collective-permute-start.12 = (bf16[2,2560]{1,0:T(2,128)(2,1)S(1)}, bf16[2,2560]{1,0:T(2,128)(2,1)S(1)}, u32[]{:S(2)}, u32[]{:S(2)}) collective-permute-start(bf16[2,2560]{1,0:T(2,128)(2,1)S(1)} %collective-permute-done.11), channel_id=1, source_target_pairs={{0,4},{4,8},{8,12},{12,16},{16,20},{20,24},{24,28},{28,0},{1,5},{5... | collective-permute-start | bytes 30728 | tf_op jit(solution)/shard_map/ppermute | solution.py:108
  170.9 171.2 %collective-permute-start.15 = (f32[2]{0:T(128)S(1)}, f32[2]{0:T(128)S(1)}, u32[]{:S(2)}, u32[]{:S(2)}) collective-permute-start(f32[2]{0:T(128)S(1)} %slice_convert_fusion), channel_id=1, source_target_pairs={{2,0},{3,1},{6,4},{7,5},{10,8},{11,9},{14,12},{15,13},{18,16},{19,... | collective-permute-start | bytes 32 | tf_op jit(solution)/shard_map/ppermute | solution.py:15
  176.7 6.4 %collective-permute-start.13 = (bf16[2,2560]{1,0:T(2,128)(2,1)S(1)}, bf16[2,2560]{1,0:T(2,128)(2,1)S(1)}, u32[]{:S(2)}, u32[]{:S(2)}) collective-permute-start(bf16[2,2560]{1,0:T(2,128)(2,1)S(1)} %collective-permute-done.12), channel_id=1, source_target_pairs={{0,4},{4,8},{8,12},{12,16},{16,20},{20,24},{24,28},{28,0},{1,5},{5... | collective-permute-start | bytes 30728 | tf_op jit(solution)/shard_map/ppermute | solution.py:108
  183.1 6.4 %collective-permute-start.14 = (bf16[2,2560]{1,0:T(2,128)(2,1)S(1)}, bf16[2,2560]{1,0:T(2,128)(2,1)S(1)}, u32[]{:S(2)}, u32[]{:S(2)}) collective-permute-start(bf16[2,2560]{1,0:T(2,128)(2,1)S(1)} %collective-permute-done.13), channel_id=1, source_target_pairs={{0,4},{4,8},{8,12},{12,16},{16,20},{20,24},{24,28},{28,0},{1,5},{5... | collective-permute-start | bytes 30728 | tf_op jit(solution)/shard_map/ppermute | solution.py:108
  189.8 93.3 %copy-start.4 = (pred[2]{0:T(512)(128)(4,1)S(1)}, pred[2]{0:T(512)(128)(4,1)}, u32[]{:S(2)}) copy-start(pred[2]{0:T(512)(128)(4,1)} %copy-done.3) | copy-start | bytes 10
  214.7 194.3 %all-reduce.17.cloned.1.call-start = ((), (), s32[]{:S(2)}) async-start(), calls=%async_computation.3 | async-start | bytes 163840
  342.1 115.3 %all-reduce.11.cloned.1.call-start = ((), (), s32[]{:S(2)}) async-start(), calls=%async_computation | async-start | bytes 327680 | tf_op jit(solution)/shard_map/psum | solution.py:207
  410.9 3.1 collective-permute-start.16
Sparse Core Ops, SparseCore 0:
  66.6 69.4 all-reduce.12
  214.8 68.2 all-reduce.14
  342.2 66.7 all-reduce.16
  438.1 19.1 all-reduce.10
